TPU v7x, 32 devices: a whole 2x2x4 slice. The times are simulated.
32 devices in a mesh: band: 2 (over core), plane: 16 (over z, y, x).
Axes of the slice: x: 2, y: 2, z: 4, core: 2. Of those that a mesh axis runs over, the one named last changes fastest.
Arguments:
- bands: float32 [8, 128, 128, 128], P('band', 'plane'), may hold values from -6 to 6
- plan: int32 [2], replicated, may hold values from 0 to 7
Outputs:
- exchange_part: float32 [8, 128, 128, 128], P('band', 'plane')
All inputs are finite; a program needn't handle non-finite values.
Results may differ from a plain program's by a relative error of at most 0.00011.
Values sent between devices are 32-bit elements; how exact they have to be, the bound alone decides.
No kernel may reach another device: no remote copies, remote signals or barrier semaphores. Data moves between devices by JAX's collectives and lax.ppermute only.
A program may use at most 64 MiB of HBM per device.

v0:
```python
import math
import jax
import jax.numpy as jnp
from jax import lax
from jax.sharding import PartitionSpec as P

screening = 0.1
highest = lax.Precision.HIGHEST


def spread(value, axis, source):
    kept = jnp.where(lax.axis_index(axis) == source, value, 0).astype(value.dtype)
    return lax.psum(kept, axis)


def tables(points, retained):
    lowest = jnp.arange(retained // 2, dtype=jnp.int32)
    spectral = jnp.concatenate([lowest, lowest - retained // 2])
    where_grid = jnp.arange(points, dtype=jnp.int32)
    phases = spectral[:, None] * where_grid[None, :] % points
    angles = phases.astype(jnp.float32) * (2.0 * math.pi / points)
    return (jnp.cos(angles), jnp.sin(angles), spectral)


def coulomb(spectral, points):
    squared = (
        spectral[:, None, None] ** 2 + spectral[None, :, None] ** 2 + spectral[None, None, :] ** 2
    )
    spacing = 2.0 * math.pi / points
    values = 1.0 / (spacing * spacing * squared.astype(jnp.float32) + screening * screening)
    return jnp.where(squared < (points // 4) ** 2, values, 0.0)


def along_last(values, table):
    return jnp.einsum("bxyz,kz->bxyk", values, table, precision=highest)


def back_last(values, table):
    return jnp.einsum("bxyk,kz->bxyz", values, table, precision=highest)


def along_rows(values, table):
    return jnp.einsum("bxyk,jy->bxjk", values, table, precision=highest)


def back_rows(values, table):
    return jnp.einsum("bxjk,jy->bxyk", values, table, precision=highest)


def along_planes(values, table):
    return jnp.einsum("bxsc,kx->bksc", values, table, precision=highest)


def back_planes(values, table):
    return jnp.einsum("bksc,kx->bxsc", values, table, precision=highest)


def per_device(bands, plan):
    local_count, planes, points = (bands.shape[0], bands.shape[1], bands.shape[2])
    plane_count = lax.axis_size("plane")
    cos_table, sin_table, spectral = tables(points, points)
    share = points // plane_count
    kernel_full = coulomb(spectral, points).reshape(points, points * points)
    kernel_mine = lax.dynamic_slice_in_dim(
        kernel_full, lax.axis_index("plane") * (share * points), share * points, 1
    )
    kernel_mine = kernel_mine[:, None, :]
    scale_back = 1.0 / float(points) ** 3
    accumulated = jnp.zeros(bands.shape, jnp.float32)
    for turn_index in range(plan.shape[0]):
        chosen = plan[turn_index]
        own_band = lax.dynamic_index_in_dim(bands, chosen % local_count, 0, keepdims=False)
        partner = spread(own_band, "band", chosen // local_count)
        density = partner[None] * bands
        potentials_real_part = along_last(density, cos_table)
        potentials_imag_part = -along_last(density, sin_table)
        row_real = along_rows(potentials_real_part, cos_table) + along_rows(
            potentials_imag_part, sin_table
        )
        row_imag = along_rows(potentials_imag_part, cos_table) - along_rows(
            potentials_real_part, sin_table
        )
        items = density.shape[0]
        shaped = (items, planes, plane_count, share * points)
        real_part = lax.all_to_all(
            row_real.reshape(shaped), "plane", split_axis=2, concat_axis=1, tiled=True
        )
        imag_part = lax.all_to_all(
            row_imag.reshape(shaped), "plane", split_axis=2, concat_axis=1, tiled=True
        )
        fwd_real = along_planes(real_part, cos_table) + along_planes(imag_part, sin_table)
        fwd_imag = along_planes(imag_part, cos_table) - along_planes(real_part, sin_table)
        fwd_real = fwd_real * kernel_mine
        fwd_imag = fwd_imag * kernel_mine
        back_real = back_planes(fwd_real, cos_table) - back_planes(fwd_imag, sin_table)
        back_imag = back_planes(fwd_real, sin_table) + back_planes(fwd_imag, cos_table)
        out_real = lax.all_to_all(back_real, "plane", split_axis=1, concat_axis=2, tiled=True)
        out_imag = lax.all_to_all(back_imag, "plane", split_axis=1, concat_axis=2, tiled=True)
        out_real = out_real.reshape(items, planes, points, points)
        out_imag = out_imag.reshape(items, planes, points, points)
        col_real = back_rows(out_real, cos_table) - back_rows(out_imag, sin_table)
        col_imag = back_rows(out_real, sin_table) + back_rows(out_imag, cos_table)
        first_back = (back_last(col_real, cos_table) - back_last(col_imag, sin_table)) * scale_back
        accumulated = accumulated - partner[None] * first_back
    return accumulated


def solution(mesh):
    in_specs = (P("band", "plane", None, None), P())
    out_specs = P("band", "plane", None, None)
    return jax.shard_map(
        per_device, mesh=mesh, in_specs=in_specs, out_specs=out_specs, check_vma=False
    )
```

profile of v0, /device:TPU:12, one launch (start us, length us, event | category | flops | bytes accessed | tf_op | source)
XLA Modules:
  0.0 505.0 jit_solution(16058967309255782225)
XLA Ops:
  15.7 21.1 %all-reduce.3.cloned.1.call-done = (f32[8,128,128]{2,1,0:T(8,128)}, f32[8,128,128]{2,1,0:T(8,128)}) async-done(((f32[8,128,128]{2,1,0:T(8,128)}, f32[8,128,128]{2,1,0:T(8,128)}), (f32[8,128,128]{2,1,0:T(8,128)}, f32[8,128,128]{2,1,0:T(8,128)})) %all-reduce.3.cloned.1.call-update) | async-done | bytes 1048592 | tf_op jit(solution)/shard_map/psum | solution.py:13
  50.8 4.1 copy.33
  54.9 7.3 %all-to-all-start.1 = ((f32[4,8,16,1024]{3,1,0,2:T(8,128)}), f32[4,8,16,1024]{3,1,0,2:T(8,128)}, u32[]{:S(2)}, u32[]{:S(2)}) async-start(f32[4,8,16,1024]{3,1,0,2:T(8,128)} %copy.33), calls=%async_computation.1 | async-start | bytes 4194304 | tf_op jit(solution)/shard_map/all_to_all | solution.py:88
  62.2 3.9 fusion.148
  72.4 4.2 copy.31
  76.6 33.9 %all-to-all-done.1 = f32[4,8,16,1024]{3,1,0,2:T(8,128)} async-done(((f32[4,8,16,1024]{3,1,0,2:T(8,128)}), f32[4,8,16,1024]{3,1,0,2:T(8,128)}, u32[]{:S(2)}, u32[]{:S(2)}) %all-to-all-start.1) | async-done | bytes 2097184 | tf_op jit(solution)/shard_map/all_to_all | solution.py:88
  110.5 5.4 %all-to-all-start = ((f32[4,8,16,1024]{3,1,0,2:T(8,128)}), f32[4,8,16,1024]{3,1,0,2:T(8,128)}, u32[]{:S(2)}, u32[]{:S(2)}) async-start(f32[4,8,16,1024]{3,1,0,2:T(8,128)} %copy.31), calls=%async_computation | async-start | bytes 4194304 | tf_op jit(solution)/shard_map/all_to_all | solution.py:85
  128.7 4.1 copy.49
  132.8 30.8 %all-to-all-done = f32[4,8,16,1024]{3,1,0,2:T(8,128)} async-done(((f32[4,8,16,1024]{3,1,0,2:T(8,128)}), f32[4,8,16,1024]{3,1,0,2:T(8,128)}, u32[]{:S(2)}, u32[]{:S(2)}) %all-to-all-start) | async-done | bytes 2097184 | tf_op jit(solution)/shard_map/all_to_all | solution.py:85
  163.6 5.2 %all-to-all-start.5 = ((f32[4,8,16,1024]{3,1,0,2:T(8,128)}), f32[4,8,16,1024]{3,1,0,2:T(8,128)}, u32[]{:S(2)}, u32[]{:S(2)}) async-start(f32[4,8,16,1024]{3,1,0,2:T(8,128)} %copy.49), calls=%async_computation.5 | async-start | bytes 4194304 | tf_op jit(solution)/shard_map/all_to_all | solution.py:88
  174.8 4.2 copy.47
  179.0 37.4 %all-to-all-done.5 = f32[4,8,16,1024]{3,1,0,2:T(8,128)} async-done(((f32[4,8,16,1024]{3,1,0,2:T(8,128)}), f32[4,8,16,1024]{3,1,0,2:T(8,128)}, u32[]{:S(2)}, u32[]{:S(2)}) %all-to-all-start.5) | async-done | bytes 2097184 | tf_op jit(solution)/shard_map/all_to_all | solution.py:88
  216.4 4.6 all-to-all-start.4
  223.7 9.8 %copy.143 = s32[16,8,128,128]{3,1,2,0:T(8,128)} copy(s32[16,8,128,128]{3,2,1,0:T(8,128)S(1)} %bitcast.314) | data formatting | bytes 16777216
  238.5 4.0 bitcast_multiply_fusion.2
  249.0 4.0 bitcast_multiply_fusion.3
  257.9 11.0 %all-to-all-done.4 = f32[4,8,16,1024]{3,1,0,2:T(8,128)} async-done(((f32[4,8,16,1024]{3,1,0,2:T(8,128)}), f32[4,8,16,1024]{3,1,0,2:T(8,128)}, u32[]{:S(2)}, u32[]{:S(2)}) %all-to-all-start.4) | async-done | bytes 2097184 | tf_op jit(solution)/shard_map/all_to_all | solution.py:85
  268.8 4.5 all-to-all-start.2
  282.1 38.9 %all-to-all-done.2 = f32[4,128,1,1024]{3,0,2,1:T(4,128)} async-done(((f32[4,128,1,1024]{3,0,2,1:T(4,128)}), f32[4,128,1,1024]{3,0,2,1:T(4,128)}, u32[]{:S(2)}, u32[]{:S(2)}) %all-to-all-start.2) | async-done | bytes 2097184 | tf_op jit(solution)/shard_map/all_to_all | solution.py:97
  321.0 4.6 all-to-all-start.3
  329.4 4.0 bitcast_multiply_fusion
  339.4 4.0 bitcast_multiply_fusion.1
  348.8 24.1 %all-to-all-done.3 = f32[4,128,1,1024]{3,0,2,1:T(4,128)} async-done(((f32[4,128,1,1024]{3,0,2,1:T(4,128)}), f32[4,128,1,1024]{3,0,2,1:T(4,128)}, u32[]{:S(2)}, u32[]{:S(2)}) %all-to-all-start.3) | async-done | bytes 2097184 | tf_op jit(solution)/shard_map/all_to_all | solution.py:98
  372.9 4.6 all-to-all-start.7
  386.3 38.5 %all-to-all-done.7 = f32[4,128,1,1024]{3,0,2,1:T(4,128)} async-done(((f32[4,128,1,1024]{3,0,2,1:T(4,128)}), f32[4,128,1,1024]{3,0,2,1:T(4,128)}, u32[]{:S(2)}, u32[]{:S(2)}) %all-to-all-start.7) | async-done | bytes 2097184 | tf_op jit(solution)/shard_map/all_to_all | solution.py:98
  424.8 4.7 all-to-all-start.6
  430.4 4.1 copy.147
  436.2 4.1 copy.146
  443.1 4.2 copy.144
  450.1 5.3 %fusion.139 = f32[128,4,8,128]{3,0,2,1:T(8,128)} fusion(f32[4,8,128,128]{3,2,1,0:T(8,128)} %reshape.182, s32[128]{0:T(128)S(1)} %get-tuple-element.8), kind=kOutput, calls=%fused_computation.140 | convolution fusion | flops 805535744 | bytes 4194816 | tf_op jit(solution)/shard_map/bxjk,jy->bxyk/dot_general | solution.py:47
  476.7 4.1 copy.145
  493.8 3.9 multiply_subtract_fusion
  (102 shorter events, 136.6 us)
Async XLA Ops:
  6.5 30.3 %copy-start = (f32[4,8,128,128]{3,2,1,0:T(8,128)S(1)}, f32[4,8,128,128]{3,2,1,0:T(8,128)}, u32[]{:S(2)}) copy-start(f32[4,8,128,128]{3,2,1,0:T(8,128)} %param.2) | copy-start | bytes 6291460
  6.5 30.3 %all-reduce.3.cloned.1.call-start = ((), (), s32[]{:S(2)}) async-start(), calls=%async_computation.8 | async-start | bytes 2097152 | tf_op jit(solution)/shard_map/psum | solution.py:13
  36.8 3.3 copy-start.19
  40.1 2.1 copy-start.7
  42.3 2.2 copy-start.3
  54.9 55.6 %all-to-all-start.1 = ((f32[4,8,16,1024]{3,1,0,2:T(8,128)}), f32[4,8,16,1024]{3,1,0,2:T(8,128)}, u32[]{:S(2)}, u32[]{:S(2)}) async-start(f32[4,8,16,1024]{3,1,0,2:T(8,128)} %copy.33), calls=%async_computation.1 | async-start | bytes 4194304 | tf_op jit(solution)/shard_map/all_to_all | solution.py:88
  62.2 3.9 copy-start.4
  76.6 39.2 %copy-start.18 = (f32[8,128,128]{2,1,0:T(8,128)S(1)}, f32[8,128,128]{2,1,0:T(8,128)}, u32[]{:S(2)}) copy-start(f32[8,128,128]{2,1,0:T(8,128)} %get-tuple-element.5) | copy-start | bytes 1572868
  110.5 53.2 %all-to-all-start = ((f32[4,8,16,1024]{3,1,0,2:T(8,128)}), f32[4,8,16,1024]{3,1,0,2:T(8,128)}, u32[]{:S(2)}, u32[]{:S(2)}) async-start(f32[4,8,16,1024]{3,1,0,2:T(8,128)} %copy.31), calls=%async_computation | async-start | bytes 4194304 | tf_op jit(solution)/shard_map/all_to_all | solution.py:85
  118.0 1.3 copy-start.5
  123.7 1.4 copy-start.1
  132.8 36.1 %copy-start.6 = (f32[4,8,128,128]{3,2,1,0:T(8,128)S(1)}, f32[4,8,128,128]{3,2,1,0:T(8,128)}, u32[]{:S(2)}) copy-start(f32[4,8,128,128]{3,2,1,0:T(8,128)} %copy-done.5) | copy-start | bytes 6291460
  163.6 52.7 %all-to-all-start.5 = ((f32[4,8,16,1024]{3,1,0,2:T(8,128)}), f32[4,8,16,1024]{3,1,0,2:T(8,128)}, u32[]{:S(2)}, u32[]{:S(2)}) async-start(f32[4,8,16,1024]{3,1,0,2:T(8,128)} %copy.49), calls=%async_computation.5 | async-start | bytes 4194304 | tf_op jit(solution)/shard_map/all_to_all | solution.py:88
  168.9 2.2 copy-start.2
  216.4 52.4 %all-to-all-start.4 = ((f32[4,8,16,1024]{3,1,0,2:T(8,128)}), f32[4,8,16,1024]{3,1,0,2:T(8,128)}, u32[]{:S(2)}, u32[]{:S(2)}) async-start(f32[4,8,16,1024]{3,1,0,2:T(8,128)} %copy.47), calls=%async_computation.4 | async-start | bytes 4194304 | tf_op jit(solution)/shard_map/all_to_all | solution.py:85
  242.5 2.7 copy-start.9
  268.8 52.1 %all-to-all-start.2 = ((f32[4,128,1,1024]{3,0,2,1:T(4,128)}), f32[4,128,1,1024]{3,0,2,1:T(4,128)}, u32[]{:S(2)}, u32[]{:S(2)}) async-start(f32[4,128,1,1024]{3,0,2,1:T(4,128)} %copy.37), calls=%async_computation.2 | async-start | bytes 4194304 | tf_op jit(solution)/shard_map/all_to_all | solution.py:97
  321.0 51.9 %all-to-all-start.3 = ((f32[4,128,1,1024]{3,0,2,1:T(4,128)}), f32[4,128,1,1024]{3,0,2,1:T(4,128)}, u32[]{:S(2)}, u32[]{:S(2)}) async-start(f32[4,128,1,1024]{3,0,2,1:T(4,128)} %copy.42), calls=%async_computation.3 | async-start | bytes 4194304 | tf_op jit(solution)/shard_map/all_to_all | solution.py:98
  333.4 2.2 copy-start.8
  372.9 51.8 %all-to-all-start.7 = ((f32[4,128,1,1024]{3,0,2,1:T(4,128)}), f32[4,128,1,1024]{3,0,2,1:T(4,128)}, u32[]{:S(2)}, u32[]{:S(2)}) async-start(f32[4,128,1,1024]{3,0,2,1:T(4,128)} %copy.58), calls=%async_computation.7 | async-start | bytes 4194304 | tf_op jit(solution)/shard_map/all_to_all | solution.py:98
  386.3 43.2 %copy-start.20 = (f32[8,128,128]{2,1,0:T(8,128)S(1)}, f32[8,128,128]{2,1,0:T(8,128)}, u32[]{:S(2)}) copy-start(f32[8,128,128]{2,1,0:T(8,128)} %get-tuple-element.6) | copy-start | bytes 1572868
  424.8 51.9 %all-to-all-start.6 = ((f32[4,128,1,1024]{3,0,2,1:T(4,128)}), f32[4,128,1,1024]{3,0,2,1:T(4,128)}, u32[]{:S(2)}, u32[]{:S(2)}) async-start(f32[4,128,1,1024]{3,0,2,1:T(4,128)} %copy.53), calls=%async_computation.6 | async-start | bytes 4194304 | tf_op jit(solution)/shard_map/all_to_all | solution.py:97
  450.1 5.3 %copy-start.11 = (f32[4,8,128,128]{3,2,1,0:T(8,128)S(1)}, f32[4,8,128,128]{3,2,1,0:T(8,128)}, u32[]{:S(2)}) copy-start(f32[4,8,128,128]{3,2,1,0:T(8,128)} %reshape.182) | copy-start | bytes 6291460
  462.6 3.6 copy-start.10
  485.0 2.3 copy-start.13
  485.0 2.3 copy-start.16
  487.2 2.2 copy-start.12
  487.2 2.2 copy-start.14
  489.5 2.2 copy-start.15
  491.6 2.2 copy-start.17
  491.6 2.2 copy-start.21
Sparse Core Ops, SparseCore 0:
  15.8 21.0 all-reduce.2
where the time goes:
time: 514 us; the launch traced here: 505 us
  waiting for transfers between devices  239 us (46%)
  matrix products  123 us (24%)
  local copies, waits for them, and re-layouts  78.2 us (15%)
  starting transfers between devices  40.9 us (8%)
  between operations  19.7 us (4%)
    all_to_all x2, waiting for transfers between devices, per_device(): lax.all_to_all(row_imag.reshape(shaped), 'plane', split_axis=2, concat_ax...  71.3 us
    all_to_all x2, waiting for transfers between devices, per_device(): lax.all_to_all(back_imag, 'plane', split_axis=1, concat_axis=2, tiled=True)  62.6 us
    all_to_all x2, waiting for transfers between devices, per_device(): lax.all_to_all(back_real, 'plane', split_axis=1, concat_axis=2, tiled=True)  42.3 us
    all_to_all x2, waiting for transfers between devices, per_device(): lax.all_to_all(row_real.reshape(shaped), 'plane', split_axis=2, concat_ax...  41.8 us
    dot_general x8, matrix products, along_planes(): return jnp.einsum('bxsc,kx->bksc', values, table, precision=highest)  31.1 us
    dot_general x8, matrix products, back_rows(): return jnp.einsum('bxjk,jy->bxyk', values, table, precision=highest)  27.6 us
    dot_general x8, matrix products, back_planes(): return jnp.einsum('bksc,kx->bxsc', values, table, precision=highest)  21.9 us
    dot_general x8, matrix products, along_rows(): return jnp.einsum('bxyk,jy->bxjk', values, table, precision=highest)  21.9 us
  transfers between devices with their start and end apart: 9, of which 9 were waited for; matrix products, arithmetic and copies ran while one was open for 32% of the time, Pallas kernels for 0%

commit v1 on v0

--- a/solution.py
+++ b/solution.py
@@ -10,7 +10,7 @@
 
 def spread(value, axis, source):
     kept = jnp.where(lax.axis_index(axis) == source, value, 0).astype(value.dtype)
-    return lax.psum(kept, axis)
+    return jnp.sum(lax.all_gather(kept, axis), axis=0)
 
 
 def tables(points, retained):

time: 514 us -> 504 us (0.981)
  waiting for transfers between devices: 239 us -> 229 us
    all_gather x0 -> x2, waiting for transfers between devices: none -> 22.3 us  [spread(): return jnp.sum(lax.all_gather(kept, axis), axis=0)]
    psum x1 -> x0, waiting for transfers between devices: 21.1 us -> none  [spread(): return lax.psum(kept, axis)]
    all_to_all x2, waiting for transfers between devices: 62.6 us -> 77.4 us  [per_device(): lax.all_to_all(back_imag, 'plane', split_axis=1, concat_axis=2, tiled=True)]
    all_to_all x2, waiting for transfers between devices: 41.8 us -> 27.9 us  [per_device(): lax.all_to_all(row_real.reshape(shaped), 'plane', split_axis=2, concat_ax...]
    all_to_all x2, waiting for transfers between devices: 42.3 us -> 29.1 us  [per_device(): lax.all_to_all(back_real, 'plane', split_axis=1, concat_axis=2, tiled=True)]
    unnamed x45 -> x43, local copies, waits for them, and re-layouts: 12.6 us -> 12.6 us
  transfers between devices with their start and end apart: 9 -> 10, of which waited for: 9 -> 10; matrix products, arithmetic and copies ran while one was open for 32% -> 32% of each run, Pallas kernels for 0% -> 0%
where the time goes in v1:
time: 504 us; the launch traced here: 494 us
  waiting for transfers between devices  229 us (45%)
  matrix products  120 us (24%)
  local copies, waits for them, and re-layouts  78.3 us (16%)
  starting transfers between devices  41 us (8%)
  between operations  19.6 us (4%)
  other arithmetic  7.31 us (1%)
    all_to_all x2, waiting for transfers between devices, per_device(): lax.all_to_all(back_imag, 'plane', split_axis=1, concat_axis=2, tiled=True)  77.4 us
    all_to_all x2, waiting for transfers between devices, per_device(): lax.all_to_all(row_imag.reshape(shaped), 'plane', split_axis=2, concat_ax...  71.3 us
    dot_general x8, matrix products, along_planes(): return jnp.einsum('bxsc,kx->bksc', values, table, precision=highest)  30.9 us
    all_to_all x2, waiting for transfers between devices, per_device(): lax.all_to_all(back_real, 'plane', split_axis=1, concat_axis=2, tiled=True)  29.1 us
    all_to_all x2, waiting for transfers between devices, per_device(): lax.all_to_all(row_real.reshape(shaped), 'plane', split_axis=2, concat_ax...  27.9 us
    dot_general x8, matrix products, back_rows(): return jnp.einsum('bxjk,jy->bxyk', values, table, precision=highest)  25.9 us
    all_gather x2, waiting for transfers between devices, spread(): return jnp.sum(lax.all_gather(kept, axis), axis=0)  22.3 us
    dot_general x8, matrix products, back_planes(): return jnp.einsum('bksc,kx->bxsc', values, table, precision=highest)  21.9 us
  transfers between devices with their start and end apart: 10, of which 10 were waited for; matrix products, arithmetic and copies ran while one was open for 32% of the time, Pallas kernels for 0%

profile of v1, /device:TPU:12, one launch (start us, length us, event | category | flops | bytes accessed | tf_op | source)
XLA Modules:
  0.0 494.5 jit_solution(18365692164600785927)
XLA Ops:
  15.6 10.5 %all-gather.3.cloned.1.call-done = f32[2,8,128,128]{3,2,1,0:T(8,128)} async-done(((f32[1,8,128,128]{3,2,1,0:T(8,128)}), f32[2,8,128,128]{3,2,1,0:T(8,128)}) %all-gather.3.cloned.1.call-update) | async-done | bytes 1048592 | tf_op jit(solution)/shard_map/all_gather | solution.py:13
  40.2 4.1 copy.33
  44.3 7.3 %all-to-all-start.1 = ((f32[4,8,16,1024]{3,1,0,2:T(8,128)}), f32[4,8,16,1024]{3,1,0,2:T(8,128)}, u32[]{:S(2)}, u32[]{:S(2)}) async-start(f32[4,8,16,1024]{3,1,0,2:T(8,128)} %copy.33), calls=%async_computation.1 | async-start | bytes 4194304 | tf_op jit(solution)/shard_map/all_to_all | solution.py:88
  51.7 3.9 fusion.148
  61.9 4.2 copy.31
  66.0 33.9 %all-to-all-done.1 = f32[4,8,16,1024]{3,1,0,2:T(8,128)} async-done(((f32[4,8,16,1024]{3,1,0,2:T(8,128)}), f32[4,8,16,1024]{3,1,0,2:T(8,128)}, u32[]{:S(2)}, u32[]{:S(2)}) %all-to-all-start.1) | async-done | bytes 2097184 | tf_op jit(solution)/shard_map/all_to_all | solution.py:88
  99.9 5.4 %all-to-all-start = ((f32[4,8,16,1024]{3,1,0,2:T(8,128)}), f32[4,8,16,1024]{3,1,0,2:T(8,128)}, u32[]{:S(2)}, u32[]{:S(2)}) async-start(f32[4,8,16,1024]{3,1,0,2:T(8,128)} %copy.31), calls=%async_computation | async-start | bytes 4194304 | tf_op jit(solution)/shard_map/all_to_all | solution.py:85
  106.1 11.8 %all-gather.5.cloned.1.call-done = f32[2,8,128,128]{3,2,1,0:T(8,128)} async-done(((f32[1,8,128,128]{3,2,1,0:T(8,128)}), f32[2,8,128,128]{3,2,1,0:T(8,128)}) %all-gather.5.cloned.1.call-update) | async-done | bytes 1048592 | tf_op jit(solution)/shard_map/all_gather | solution.py:13
  132.1 4.1 copy.49
  136.3 16.9 %all-to-all-done = f32[4,8,16,1024]{3,1,0,2:T(8,128)} async-done(((f32[4,8,16,1024]{3,1,0,2:T(8,128)}), f32[4,8,16,1024]{3,1,0,2:T(8,128)}, u32[]{:S(2)}, u32[]{:S(2)}) %all-to-all-start) | async-done | bytes 2097184 | tf_op jit(solution)/shard_map/all_to_all | solution.py:85
  153.2 5.2 %all-to-all-start.5 = ((f32[4,8,16,1024]{3,1,0,2:T(8,128)}), f32[4,8,16,1024]{3,1,0,2:T(8,128)}, u32[]{:S(2)}, u32[]{:S(2)}) async-start(f32[4,8,16,1024]{3,1,0,2:T(8,128)} %copy.49), calls=%async_computation.5 | async-start | bytes 4194304 | tf_op jit(solution)/shard_map/all_to_all | solution.py:88
  164.4 4.2 copy.47
  168.5 37.4 %all-to-all-done.5 = f32[4,8,16,1024]{3,1,0,2:T(8,128)} async-done(((f32[4,8,16,1024]{3,1,0,2:T(8,128)}), f32[4,8,16,1024]{3,1,0,2:T(8,128)}, u32[]{:S(2)}, u32[]{:S(2)}) %all-to-all-start.5) | async-done | bytes 2097184 | tf_op jit(solution)/shard_map/all_to_all | solution.py:88
  205.9 4.6 all-to-all-start.4
  213.3 9.8 %copy.143 = s32[16,8,128,128]{3,1,2,0:T(8,128)} copy(s32[16,8,128,128]{3,2,1,0:T(8,128)S(1)} %bitcast.310) | data formatting | bytes 16777216
  228.1 4.0 bitcast_multiply_fusion.2
  238.5 4.0 bitcast_multiply_fusion.3
  247.4 11.0 %all-to-all-done.4 = f32[4,8,16,1024]{3,1,0,2:T(8,128)} async-done(((f32[4,8,16,1024]{3,1,0,2:T(8,128)}), f32[4,8,16,1024]{3,1,0,2:T(8,128)}, u32[]{:S(2)}, u32[]{:S(2)}) %all-to-all-start.4) | async-done | bytes 2097184 | tf_op jit(solution)/shard_map/all_to_all | solution.py:85
  258.4 4.5 all-to-all-start.3
  271.7 38.9 %all-to-all-done.3 = f32[4,128,1,1024]{3,0,2,1:T(4,128)} async-done(((f32[4,128,1,1024]{3,0,2,1:T(4,128)}), f32[4,128,1,1024]{3,0,2,1:T(4,128)}, u32[]{:S(2)}, u32[]{:S(2)}) %all-to-all-start.3) | async-done | bytes 2097184 | tf_op jit(solution)/shard_map/all_to_all | solution.py:98
  310.5 4.7 all-to-all-start.2
  318.9 4.0 bitcast_multiply_fusion
  328.9 4.0 bitcast_multiply_fusion.1
  338.3 24.1 %all-to-all-done.2 = f32[4,128,1,1024]{3,0,2,1:T(4,128)} async-done(((f32[4,128,1,1024]{3,0,2,1:T(4,128)}), f32[4,128,1,1024]{3,0,2,1:T(4,128)}, u32[]{:S(2)}, u32[]{:S(2)}) %all-to-all-start.2) | async-done | bytes 2097184 | tf_op jit(solution)/shard_map/all_to_all | solution.py:97
  362.4 4.6 all-to-all-start.7
  375.8 38.5 %all-to-all-done.7 = f32[4,128,1,1024]{3,0,2,1:T(4,128)} async-done(((f32[4,128,1,1024]{3,0,2,1:T(4,128)}), f32[4,128,1,1024]{3,0,2,1:T(4,128)}, u32[]{:S(2)}, u32[]{:S(2)}) %all-to-all-start.7) | async-done | bytes 2097184 | tf_op jit(solution)/shard_map/all_to_all | solution.py:98
  414.3 4.7 all-to-all-start.6
  419.8 4.2 copy.146
  425.7 4.2 copy.147
  432.7 4.1 copy.144
  461.2 4.9 all-to-all-done.6
  466.2 4.1 copy.145
  (106 shorter events, 143.1 us)
Async XLA Ops:
  6.5 19.5 %all-gather.3.cloned.1.call-start = ((), (), s32[]{:S(2)}) async-start(), calls=%async_computation.8 | async-start | bytes 1572864 | tf_op jit(solution)/shard_map/all_gather | solution.py:13
  13.1 14.4 %copy-start = (f32[4,8,128,128]{3,2,1,0:T(8,128)S(1)}, f32[4,8,128,128]{3,2,1,0:T(8,128)}, u32[]{:S(2)}) copy-start(f32[4,8,128,128]{3,2,1,0:T(8,128)} %param.2) | copy-start | bytes 6291460
  29.6 2.2 copy-start.7
  31.7 2.2 copy-start.3
  44.3 55.6 %all-to-all-start.1 = ((f32[4,8,16,1024]{3,1,0,2:T(8,128)}), f32[4,8,16,1024]{3,1,0,2:T(8,128)}, u32[]{:S(2)}, u32[]{:S(2)}) async-start(f32[4,8,16,1024]{3,1,0,2:T(8,128)} %copy.33), calls=%async_computation.1 | async-start | bytes 4194304 | tf_op jit(solution)/shard_map/all_to_all | solution.py:88
  51.7 3.9 copy-start.4
  99.9 53.3 %all-to-all-start = ((f32[4,8,16,1024]{3,1,0,2:T(8,128)}), f32[4,8,16,1024]{3,1,0,2:T(8,128)}, u32[]{:S(2)}, u32[]{:S(2)}) async-start(f32[4,8,16,1024]{3,1,0,2:T(8,128)} %copy.31), calls=%async_computation | async-start | bytes 4194304 | tf_op jit(solution)/shard_map/all_to_all | solution.py:85
  105.4 12.6 %all-gather.5.cloned.1.call-start = ((), (), s32[]{:S(2)}) async-start(), calls=%async_computation.9 | async-start | bytes 1572864 | tf_op jit(solution)/shard_map/all_gather | solution.py:13
  119.3 5.7 %copy-start.17 = (f32[8,128,128]{2,1,0:T(8,128)}, f32[8,128,128]{2,1,0:T(8,128)S(1)}, u32[]{:S(2)}) copy-start(f32[8,128,128]{2,1,0:T(8,128)S(1)} %reduce_sum.19) | copy-start | bytes 1572868
  121.4 1.3 copy-start.5
  127.1 1.4 copy-start.1
  136.3 22.2 %copy-start.6 = (f32[4,8,128,128]{3,2,1,0:T(8,128)S(1)}, f32[4,8,128,128]{3,2,1,0:T(8,128)}, u32[]{:S(2)}) copy-start(f32[4,8,128,128]{3,2,1,0:T(8,128)} %copy-done.5) | copy-start | bytes 6291460
  153.2 52.8 %all-to-all-start.5 = ((f32[4,8,16,1024]{3,1,0,2:T(8,128)}), f32[4,8,16,1024]{3,1,0,2:T(8,128)}, u32[]{:S(2)}, u32[]{:S(2)}) async-start(f32[4,8,16,1024]{3,1,0,2:T(8,128)} %copy.49), calls=%async_computation.5 | async-start | bytes 4194304 | tf_op jit(solution)/shard_map/all_to_all | solution.py:88
  158.5 2.2 copy-start.2
  205.9 52.5 %all-to-all-start.4 = ((f32[4,8,16,1024]{3,1,0,2:T(8,128)}), f32[4,8,16,1024]{3,1,0,2:T(8,128)}, u32[]{:S(2)}, u32[]{:S(2)}) async-start(f32[4,8,16,1024]{3,1,0,2:T(8,128)} %copy.47), calls=%async_computation.4 | async-start | bytes 4194304 | tf_op jit(solution)/shard_map/all_to_all | solution.py:85
  232.0 2.7 copy-start.9
  258.4 52.1 %all-to-all-start.3 = ((f32[4,128,1,1024]{3,0,2,1:T(4,128)}), f32[4,128,1,1024]{3,0,2,1:T(4,128)}, u32[]{:S(2)}, u32[]{:S(2)}) async-start(f32[4,128,1,1024]{3,0,2,1:T(4,128)} %copy.42), calls=%async_computation.3 | async-start | bytes 4194304 | tf_op jit(solution)/shard_map/all_to_all | solution.py:98
  310.5 51.9 %all-to-all-start.2 = ((f32[4,128,1,1024]{3,0,2,1:T(4,128)}), f32[4,128,1,1024]{3,0,2,1:T(4,128)}, u32[]{:S(2)}, u32[]{:S(2)}) async-start(f32[4,128,1,1024]{3,0,2,1:T(4,128)} %copy.37), calls=%async_computation.2 | async-start | bytes 4194304 | tf_op jit(solution)/shard_map/all_to_all | solution.py:97
  322.9 2.2 copy-start.8
  362.4 51.8 %all-to-all-start.7 = ((f32[4,128,1,1024]{3,0,2,1:T(4,128)}), f32[4,128,1,1024]{3,0,2,1:T(4,128)}, u32[]{:S(2)}, u32[]{:S(2)}) async-start(f32[4,128,1,1024]{3,0,2,1:T(4,128)} %copy.58), calls=%async_computation.7 | async-start | bytes 4194304 | tf_op jit(solution)/shard_map/all_to_all | solution.py:98
  375.8 43.2 %copy-start.18 = (f32[8,128,128]{2,1,0:T(8,128)S(1)}, f32[8,128,128]{2,1,0:T(8,128)}, u32[]{:S(2)}) copy-start(f32[8,128,128]{2,1,0:T(8,128)} %copy-done.17) | copy-start | bytes 1572868
  414.3 51.9 %all-to-all-start.6 = ((f32[4,128,1,1024]{3,0,2,1:T(4,128)}), f32[4,128,1,1024]{3,0,2,1:T(4,128)}, u32[]{:S(2)}, u32[]{:S(2)}) async-start(f32[4,128,1,1024]{3,0,2,1:T(4,128)} %copy.53), calls=%async_computation.6 | async-start | bytes 4194304 | tf_op jit(solution)/shard_map/all_to_all | solution.py:97
  443.3 3.5 copy-start.10
  450.4 3.6 copy-start.11
  474.5 2.3 copy-start.13
  474.5 2.3 copy-start.16
  476.7 2.2 copy-start.12
  476.7 2.2 copy-start.14
  478.9 2.2 copy-start.15
  481.1 2.2 copy-start.19
  481.1 2.2 copy-start.20
Sparse Core Ops, SparseCore 0:
  15.6 10.3 all-gather.2
  107.7 10.1 all-gather.4
